TPU v7x, 128 devices: a whole 4x4x4 slice. The times are simulated.
128 devices in a mesh: seq: 16 (over y, x_lo, core), tp: 8 (over z, x_hi).
Axes of the slice: x: 4 (x_hi: 2, x_lo: 2; x = x_hi * 2 + x_lo), y: 4, z: 4, core: 2. Of those that a mesh axis runs over, the one named last changes fastest.
Arguments:
- tokens: bfloat16 [8192, 1024], P('seq', 'tp'), may hold values from -6 to 6
- variate: int32 [8192], P('seq'), may hold values from 0 to 3
- positions: int32 [8192], P('seq'), may hold values from 0 to 511
- lengths: int32 [4], replicated, may hold values from 1 to 4096, 8192 in all
- page_table: int32 [144], replicated, may hold values from 0 to 143, each once
- gain_attn: bfloat16 [1024], replicated, may hold values from 0.099609375 to 1.8984375
- w_query: bfloat16 [1024, 1024], P(None, 'tp'), may hold values from -1 to 1
- w_key: bfloat16 [1024, 1024], P(None, 'tp'), may hold values from -1 to 1
- w_value: bfloat16 [1024, 1024], P(None, 'tp'), may hold values from -0.1875 to 0.1875
- var_bias: float32 [2, 16], P(None, 'tp'), may hold values from -2 to 2
- w_out: bfloat16 [1024, 1024], P('tp'), may hold values from -0.1875 to 0.1875
- gain_ffn: bfloat16 [1024], replicated, may hold values from 0.099609375 to 1.8984375
- w_gate: bfloat16 [1024, 4096], P(None, 'tp'), may hold values from -0.1875 to 0.1875
- w_up: bfloat16 [1024, 4096], P(None, 'tp'), may hold values from -0.1875 to 0.1875
- w_down: bfloat16 [4096, 1024], P('tp'), may hold values from -0.09375 to 0.09375
Outputs:
- mixed: bfloat16 [8192, 1024], P('seq', 'tp')
- cache: bfloat16 [9216, 2, 1024], P('seq', None, 'tp')
Inputs may be any that keep to these rules, and one draw needn't show every extreme that they name: The lengths fill all 8192 token positions in order; some request has exactly 4096 tokens. `page_table`: each physical page appears once.
All inputs are finite; a program needn't handle non-finite values.
Results may differ from a plain program's by a relative error of at most 0.018.
Values may be sent and summed in bfloat16 or wider, within the bound.
A program may use at most 64 MiB of HBM per device.

v0:
```python
import jax
import jax.numpy as jnp
from jax import lax
from jax.sharding import PartitionSpec as P

HD = 64
PAGE = 64


def passed_along(value, axis, steps):
    count = lax.axis_size(axis)
    initial, last = (max(0, -steps), min(count, count - steps))
    return lax.ppermute(value, axis, [(source, source + steps) for source in range(initial, last)])


def root_mean_norm(values, gain):
    values = values.astype(jnp.float32)
    scale = lax.rsqrt(jnp.mean(values * values, axis=-1, keepdims=True) + 1e-06)
    return values * scale * gain.astype(jnp.float32)


def rotate(vectors, positions):
    half_dim = vectors.shape[-1] // 2
    frequency = 10000.0 ** (-jnp.arange(half_dim, dtype=jnp.float32) / half_dim)
    angles = positions.astype(jnp.float32)[:, None] * frequency[None, :]
    cosine = jnp.cos(angles)[:, None, :]
    sine_part = jnp.sin(angles)[:, None, :]
    first_half = vectors[..., :half_dim]
    second_half = vectors[..., half_dim:]
    return jnp.concatenate(
        [
            first_half * cosine - second_half * sine_part,
            second_half * cosine + first_half * sine_part,
        ],
        axis=-1,
    )


def segment_of(index, request_ends):
    return jnp.sum((index[:, None] >= request_ends[None, :]).astype(jnp.int32), axis=1)


def cache_slots(lengths, page_table, index):
    request_ends = jnp.cumsum(lengths)
    request_starts = request_ends - lengths
    page_counts = (lengths + PAGE - 1) // PAGE
    page_bases = jnp.cumsum(page_counts) - page_counts
    segment = segment_of(index, request_ends)
    chosen = segment[:, None] == jnp.arange(lengths.shape[0], dtype=jnp.int32)[None, :]
    offset_in = index - jnp.sum(jnp.where(chosen, request_starts[None, :], 0), axis=1)
    logical = jnp.sum(jnp.where(chosen, page_bases[None, :], 0), axis=1) + offset_in // PAGE
    page_ids = jnp.arange(page_table.shape[0], dtype=jnp.int32)
    physical = jnp.sum(
        jnp.where(logical[:, None] == page_ids[None, :], page_table[None, :], 0), axis=1
    )
    return physical * PAGE + offset_in % PAGE


def per_device(
    tokens,
    variate,
    positions,
    lengths,
    page_table,
    gain_attn,
    w_query,
    w_key,
    w_value,
    var_bias,
    w_out,
    gain_ffn,
    w_gate,
    w_up,
    w_down,
):
    token_rows = lax.all_gather(tokens, "tp", axis=1, tiled=True)
    tok_rows = token_rows.shape[0]
    row_first = lax.axis_index("seq") * tok_rows
    index = row_first + jnp.arange(tok_rows, dtype=jnp.int32)
    normed = root_mean_norm(token_rows, gain_attn).astype(jnp.bfloat16)
    local_heads = w_query.shape[1] // HD
    query_rows = rotate(
        jnp.dot(normed, w_query, preferred_element_type=jnp.float32).reshape(
            tok_rows, local_heads, HD
        ),
        positions,
    ).astype(jnp.bfloat16)
    key_rows = (
        rotate(
            jnp.dot(normed, w_key, preferred_element_type=jnp.float32).reshape(
                tok_rows, local_heads, HD
            ),
            positions,
        )
        .astype(jnp.bfloat16)
        .reshape(tok_rows, local_heads * HD)
    )
    value_rows = jnp.dot(normed, w_value, preferred_element_type=jnp.float32).astype(jnp.bfloat16)
    request_ends = jnp.cumsum(lengths)
    query_segment = segment_of(index, request_ends)
    bias_same = var_bias[0]
    bias_diff = var_bias[1]

    def attend(state, key_piece, offset):
        running_peak, running_total, weighted = state
        piece_keys, piece_values, piece_variate = key_piece
        piece_rows = piece_keys.shape[0]
        key_index = offset + jnp.arange(piece_rows, dtype=jnp.int32)
        key_segment = segment_of(key_index, request_ends)
        scores = jnp.einsum(
            "qhd,khd->hqk",
            query_rows,
            piece_keys.reshape(piece_rows, local_heads, HD),
            preferred_element_type=jnp.float32,
        ) * HD ** (-0.5)
        same = variate[:, None] == piece_variate[None, :]
        scores = scores + jnp.where(same[None], bias_same[:, None, None], bias_diff[:, None, None])
        visible = (
            (query_segment[:, None] == key_segment[None, :])
            & (index[:, None] >= key_index[None, :])
            & (key_index >= 0)[None, :]
        )
        scores = jnp.where(visible[None], scores, -1e30)
        new_peak = jnp.maximum(running_peak, jnp.max(scores, axis=-1))
        weights = jnp.where(visible[None], jnp.exp(scores - new_peak[..., None]), 0.0)
        rescale = jnp.exp(running_peak - new_peak)
        new_total = running_total * rescale + jnp.sum(weights, axis=-1)
        product = jnp.einsum(
            "hqk,khd->hqd",
            weights.astype(jnp.bfloat16),
            piece_values.reshape(piece_rows, local_heads, HD),
            preferred_element_type=jnp.float32,
        )
        return (new_peak, new_total, weighted * rescale[..., None] + product)

    state = (
        jnp.full((local_heads, tok_rows), -1e30, jnp.float32),
        jnp.zeros((local_heads, tok_rows), jnp.float32),
        jnp.zeros((local_heads, tok_rows, HD), jnp.float32),
    )
    state = attend(state, (key_rows, value_rows, variate), row_first)
    reach = lax.axis_size("seq") // 2
    for distance in range(1, reach + 1):
        moved = passed_along((key_rows, value_rows, variate), "seq", distance)
        state = attend(state, moved, row_first - distance * tok_rows)
    attended = (
        (state[2] / state[1][..., None])
        .transpose(1, 0, 2)
        .reshape(tok_rows, local_heads * HD)
        .astype(jnp.bfloat16)
    )
    projected = jnp.dot(attended, w_out, preferred_element_type=jnp.float32)
    shares = lax.psum_scatter(
        projected.astype(jnp.bfloat16), "tp", scatter_dimension=1, tiled=True
    ).astype(jnp.float32)
    residual_local = (tokens.astype(jnp.float32) + shares).astype(jnp.bfloat16)
    residual_full = lax.all_gather(residual_local, "tp", axis=1, tiled=True)
    normed_mid = root_mean_norm(residual_full, gain_ffn).astype(jnp.bfloat16)
    gate_part = jnp.dot(normed_mid, w_gate, preferred_element_type=jnp.float32)
    up_part = jnp.dot(normed_mid, w_up, preferred_element_type=jnp.float32)
    hidden = (jax.nn.silu(gate_part) * up_part).astype(jnp.bfloat16)
    down_part = jnp.dot(hidden, w_down, preferred_element_type=jnp.float32)
    ffn_share = lax.psum_scatter(
        down_part.astype(jnp.bfloat16), "tp", scatter_dimension=1, tiled=True
    ).astype(jnp.float32)
    mixed = (residual_local.astype(jnp.float32) + ffn_share).astype(jnp.bfloat16)
    pair_rows = jnp.concatenate([key_rows, value_rows], axis=1)
    cache_slot = cache_slots(lengths, page_table, index)
    cache_width = (tok_rows // PAGE + 1) * PAGE
    targets = jnp.arange(cache_width * lax.axis_size("seq"), dtype=jnp.int32)
    selector = (targets[:, None] == cache_slot[None, :]).astype(jnp.bfloat16)
    placed = lax.psum_scatter(
        jnp.dot(selector, pair_rows, preferred_element_type=jnp.float32).astype(jnp.bfloat16),
        "seq",
        scatter_dimension=0,
        tiled=True,
    )
    cache = placed.reshape(cache_width, 2, local_heads * HD)
    return (mixed, cache)


def solution(mesh):
    placed = (
        P("seq", "tp"),
        P("seq"),
        P("seq"),
        P(),
        P(),
        P(),
        P(None, "tp"),
        P(None, "tp"),
        P(None, "tp"),
        P(None, "tp"),
        P("tp", None),
        P(),
        P(None, "tp"),
        P(None, "tp"),
        P("tp", None),
    )
    return jax.shard_map(
        per_device,
        mesh=mesh,
        in_specs=placed,
        out_specs=(P("seq", "tp"), P("seq", None, "tp")),
        check_vma=False,
    )
```

profile of v0, /device:TPU:0, one launch (start us, length us, event | category | flops | bytes accessed | tf_op | source)
XLA Modules:
  0.0 419.0 jit_solution(5424332904961128005)
XLA Ops:
  7.3 1.4 collective-permute-start.1
  8.7 4.2 %collective-permute-start.10 = (s32[512]{0:T(512)}, s32[512]{0:T(512)S(1)}, u32[]{:S(2)}, u32[]{:S(2)}) collective-permute-start(s32[512]{0:T(512)} %param.16), channel_id=1, source_target_pairs={{0,32},{8,40},{16,48},{24,56},{32,64},{40,72},{48,80},{56,88},{64,... | collective-permute-start | bytes 6152 | tf_op jit(solution)/shard_map/ppermute | solution.py:13
  12.9 4.4 %collective-permute-start.13 = (s32[512]{0:T(512)}, s32[512]{0:T(512)S(1)}, u32[]{:S(2)}, u32[]{:S(2)}) collective-permute-start(s32[512]{0:T(512)} %param.16), channel_id=1, source_target_pairs={{0,40},{8,48},{16,56},{24,64},{32,72},{40,80},{48,88},{56,96},{64,... | collective-permute-start | bytes 6152 | tf_op jit(solution)/shard_map/ppermute | solution.py:13
  17.3 2.9 collective-permute-start.16
  20.2 1.6 collective-permute-start.19
  22.1 0.7 convert_element_type.131
  22.8 0.8 reduce-window.17
  23.7 2.2 and_and_fusion.5
  25.9 3.7 and_and_fusion
  29.9 2.2 collective-permute-start.22
  32.2 3.1 collective-permute-start.4
  35.3 1.3 collective-permute-start.7
  36.6 0.6 convert_element_type.129
  37.9 3.2 broadcast_compare_fusion
  41.1 26.5 %all-gather.3.cloned.1.call-done = bf16[512,1024]{1,0:T(8,128)(2,1)} async-done(((bf16[512,128]{1,0:T(8,128)(2,1)}), bf16[512,1024]{1,0:T(8,128)(2,1)}) %all-gather.3.cloned.1.call-update) | async-done | bytes 1048592 | tf_op jit(solution)/shard_map/all_gather | solution.py:76
  67.6 1.6 fusion.3
  69.2 1.9 fusion.142
  71.2 1.3 collective-permute-start
  72.5 4.3 %collective-permute-start.12 = (bf16[512,128]{0,1:T(8,128)(2,1)S(1)}, bf16[512,128]{0,1:T(8,128)(2,1)S(1)}, u32[]{:S(2)}, u32[]{:S(2)}) collective-permute-start(bf16[512,128]{0,1:T(8,128)(2,1)S(1)} %bitcast.265), channel_id=1, source_target_pairs={{0,40},{8,48},{16,56},{24,64},{32,72},{40,80},{48,88},{56,96},{64,... | collective-permute-start | bytes 393224 | tf_op jit(solution)/shard_map/ppermute | solution.py:13
  76.8 3.4 collective-permute-start.9
  80.2 3.2 collective-permute-start.6
  83.3 2.5 collective-permute-start.3
  85.9 0.6 fusion.144
  86.5 0.9 fusion.149
  88.1 1.3 collective-permute-start.18
  89.9 3.9 collective-permute-start.21
  94.4 1.3 collective-permute-start.15
  96.2 3.4 collective-permute-start.5
  100.1 1.3 collective-permute-start.8
  101.9 2.3 collective-permute-start.11
  104.3 1.0 fusion.47
  105.3 3.3 collective-permute-start.14
  108.7 4.2 fusion.11
  112.9 4.4 %collective-permute-start.17 = (bf16[512,128]{0,1:T(8,128)(2,1)S(1)}, bf16[512,128]{0,1:T(8,128)(2,1)S(1)}, u32[]{:S(2)}, u32[]{:S(2)}) collective-permute-start(bf16[512,128]{0,1:T(8,128)(2,1)S(1)} %convolution_convert_fusion.2), channel_id=1, source_target_pairs={{0,48},{8,56},{16,64},{24,72},{32,80},{40,88},{48,96},{56,104},{64... | collective-permute-start | bytes 393224 | tf_op jit(solution)/shard_map/ppermute | solution.py:13
  117.3 4.5 %fusion.13 = (f32[2,512]{1,0:T(2,128)S(1)}, f32[2,512]{1,0:T(2,128)S(1)}, f32[2,512]{1,0:T(2,128)S(1)}, f32[2,512]{1,0:T(2,128)S(1)}, f32[2,512]{1,0:T(2,128)S(1)}, /*index=5*/f32[2,512,512]{1,2,0:T(8,128)S(1)}) fusion(f32[2,512,512]{1,2,0:T(8,128)S(1)} %get-tuple-element.80, f32[2,512]{1,0:T(2,128)S(1)} %get-tuple-element.43, f32[2]{0:T(128)S(1)} %get-tuple-element.73, ...), kind=kOutput, calls=%fused_computation.36 | convolution fusion | flops 82570240 | bytes 13398032 | tf_op jit(solution)/shard_map/qhd,khd->hqk/dot_general | solution.py:110
  121.8 3.2 fusion.17
  125.1 0.8 fusion.25
  125.9 1.9 collective-permute-start.20
  127.8 1.1 convolution_bitcast_fusion.6
  128.9 1.3 collective-permute-start.23
  130.2 1.1 convolution_bitcast_fusion.5
  131.3 1.4 collective-permute-start.2
  132.7 1.1 convolution_bitcast_fusion.4
  133.8 1.1 convolution_bitcast_fusion.3
  134.9 1.1 convolution_bitcast_fusion.2
  136.0 1.1 convolution_bitcast_fusion.1
  137.1 1.1 convolution_bitcast_fusion
  138.7 0.6 fusion.29
  139.3 1.2 fusion.46
  141.0 1.3 copy.53
  142.5 69.5 %reduce-scatter.10.cloned.1.call-done = bf16[128,512]{1,0:T(8,128)(2,1)} async-done(((bf16[1024,512]{1,0:T(8,128)(2,1)}), bf16[128,512]{1,0:T(8,128)(2,1)}) %reduce-scatter.10.cloned.1.call-update) | async-done | bytes 131088
  212.0 1.0 copy.54
  213.0 0.7 add_convert_fusion.1
  214.1 45.3 %all-gather.5.cloned.1.call-done = bf16[512,1024]{1,0:T(8,128)(2,1)} async-done(((bf16[512,128]{1,0:T(8,128)(2,1)}), bf16[512,1024]{1,0:T(8,128)(2,1)}) %all-gather.5.cloned.1.call-update) | async-done | bytes 1048592 | tf_op jit(solution)/shard_map/all_gather | solution.py:157
  259.4 1.5 fusion.6
  260.9 3.4 fusion.83
  264.3 2.9 convolution_convert_fusion.1
  267.3 1.3 copy.55
  269.2 4.8 %fusion.1 = bf16[9216,256]{1,0:T(8,128)(2,1)} fusion(s32[512]{0:T(512)S(1)} %fusion.101, bf16[512,128]{0,1:T(8,128)(2,1)S(1)} %convolution_convert_fusion.2, bf16[512,128]{0,1:T(8,128)(2,1)S(1)} %bitcast.272), kind=kOutput, calls=%fused_computation.2 | convolution fusion | flops 2423521280 | bytes 4982784 | tf_op jit(solution)/shard_map/dot_general | solution.py:173
  274.0 64.7 %reduce-scatter.12.cloned.1.call-done = bf16[128,512]{1,0:T(8,128)(2,1)} async-done(((bf16[1024,512]{1,0:T(8,128)(2,1)}), bf16[128,512]{1,0:T(8,128)(2,1)}) %reduce-scatter.12.cloned.1.call-update) | async-done | bytes 131088
  338.8 1.0 copy.56
  339.8 0.7 add_convert_fusion
  340.5 70.2 %reduce-scatter.8.cloned.1.call-done = bf16[576,256]{1,0:T(8,128)(2,1)} async-done(((bf16[9216,256]{1,0:T(8,128)(2,1)}), bf16[576,256]{1,0:T(8,128)(2,1)}) %reduce-scatter.8.cloned.1.call-update) | async-done | bytes 294928 | tf_op jit(solution)/shard_map/reduce_scatter | solution.py:172
  410.7 1.7 reshape.1459
  (140 shorter events, 6.4 us)
Async XLA Ops:
  7.2 257.2 %copy-start = (bf16[512,1024]{1,0:T(8,128)(2,1)S(1)}, bf16[512,1024]{1,0:T(8,128)(2,1)}, u32[]{:S(2)}) copy-start(bf16[512,1024]{1,0:T(8,128)(2,1)} %param.29) | copy-start | bytes 3145732
  7.2 22.7 %copy-start.17 = (s32[512]{0:T(512)S(1)}, s32[512]{0:T(512)}, u32[]{:S(2)}) copy-start(s32[512]{0:T(512)} %param.16) | copy-start | bytes 6148
  7.2 29.4 %copy-start.29 = (f32[2,2]{1,0:T(2,128)S(1)}, f32[2,2]{1,0:T(2,128)}, u32[]{:S(2)}) copy-start(f32[2,2]{1,0:T(2,128)} %param.24) | copy-start | bytes 52
  7.2 29.4 %copy-start.26 = (bf16[1024]{0:T(1024)(128)(2,1)S(1)}, bf16[1024]{0:T(1024)(128)(2,1)}, u32[]{:S(2)}) copy-start(bf16[1024]{0:T(1024)(128)(2,1)} %param.20) | copy-start | bytes 6148
  7.2 60.4 %all-gather.3.cloned.1.call-start = ((), (), s32[]{:S(2)}) async-start(), calls=%async_computation.3 | async-start | bytes 1179648 | tf_op jit(solution)/shard_map/all_gather | solution.py:76
  7.3 22.6 %collective-permute-start.1 = (s32[512]{0:T(512)}, s32[512]{0:T(512)S(1)}, u32[]{:S(2)}, u32[]{:S(2)}) collective-permute-start(s32[512]{0:T(512)} %param.16), channel_id=1, source_target_pairs={{0,8},{8,16},{16,24},{24,32},{32,40},{40,48},{48,56},{56,64},{64,7... | collective-permute-start | bytes 6152 | tf_op jit(solution)/shard_map/ppermute | solution.py:13
  8.7 23.5 %collective-permute-start.10 = (s32[512]{0:T(512)}, s32[512]{0:T(512)S(1)}, u32[]{:S(2)}, u32[]{:S(2)}) collective-permute-start(s32[512]{0:T(512)} %param.16), channel_id=1, source_target_pairs={{0,32},{8,40},{16,48},{24,56},{32,64},{40,72},{48,80},{56,88},{64,... | collective-permute-start | bytes 6152 | tf_op jit(solution)/shard_map/ppermute | solution.py:13
  12.9 22.4 %collective-permute-start.13 = (s32[512]{0:T(512)}, s32[512]{0:T(512)S(1)}, u32[]{:S(2)}, u32[]{:S(2)}) collective-permute-start(s32[512]{0:T(512)} %param.16), channel_id=1, source_target_pairs={{0,40},{8,48},{16,56},{24,64},{32,72},{40,80},{48,88},{56,96},{64,... | collective-permute-start | bytes 6152 | tf_op jit(solution)/shard_map/ppermute | solution.py:13
  17.3 19.9 %collective-permute-start.16 = (s32[512]{0:T(512)}, s32[512]{0:T(512)S(1)}, u32[]{:S(2)}, u32[]{:S(2)}) collective-permute-start(s32[512]{0:T(512)} %param.16), channel_id=1, source_target_pairs={{0,48},{8,56},{16,64},{24,72},{32,80},{40,88},{48,96},{56,104},{64... | collective-permute-start | bytes 6152 | tf_op jit(solution)/shard_map/ppermute | solution.py:13
  20.2 17.0 %collective-permute-start.19 = (s32[512]{0:T(512)}, s32[512]{0:T(512)S(1)}, u32[]{:S(2)}, u32[]{:S(2)}) collective-permute-start(s32[512]{0:T(512)} %param.16), channel_id=1, source_target_pairs={{0,56},{8,64},{16,72},{24,80},{32,88},{40,96},{48,104},{56,112},{6... | collective-permute-start | bytes 6152 | tf_op jit(solution)/shard_map/ppermute | solution.py:13
  21.9 190.1 %reduce-scatter.10.cloned.1.call-start = ((), (), s32[]{:S(2)}) async-start(), calls=%async_computation.6 | async-start | bytes 1179648
  23.6 2.3 copy-start.24
  29.9 7.3 %copy-start.19 = (s32[512]{0:T(512)}, s32[512]{0:T(512)S(1)}, u32[]{:S(2)}) copy-start(s32[512]{0:T(512)S(1)} %collective-permute-done.1) | copy-start | bytes 6148
  29.9 7.3 %collective-permute-start.22 = (s32[512]{0:T(512)S(1)}, s32[512]{0:T(512)S(1)}, u32[]{:S(2)}, u32[]{:S(2)}) collective-permute-start(s32[512]{0:T(512)S(1)} %copy-done.17), channel_id=1, source_target_pairs={{0,64},{8,72},{16,80},{24,88},{32,96},{40,104},{48,112},{56,120},{... | collective-permute-start | bytes 6152 | tf_op jit(solution)/shard_map/ppermute | solution.py:13
  32.2 5.1 %copy-start.20 = (s32[512]{0:T(512)}, s32[512]{0:T(512)S(1)}, u32[]{:S(2)}) copy-start(s32[512]{0:T(512)S(1)} %collective-permute-done.10) | copy-start | bytes 6148
  32.2 5.1 %collective-permute-start.4 = (s32[512]{0:T(512)S(1)}, s32[512]{0:T(512)S(1)}, u32[]{:S(2)}, u32[]{:S(2)}) collective-permute-start(s32[512]{0:T(512)S(1)} %copy-done.17), channel_id=1, source_target_pairs={{0,16},{8,24},{16,32},{24,40},{32,48},{40,56},{48,64},{56,72},{64,... | collective-permute-start | bytes 6152 | tf_op jit(solution)/shard_map/ppermute | solution.py:13
  35.3 2.0 copy-start.21
  35.3 2.6 collective-permute-start.7
  37.2 0.6 copy-start.22
  37.2 0.6 copy-start.23
  67.6 18.3 %copy-start.2 = (bf16[512,1024]{1,0:T(8,128)(2,1)S(1)}, bf16[512,1024]{1,0:T(8,128)(2,1)}, u32[]{:S(2)}) copy-start(bf16[512,1024]{1,0:T(8,128)(2,1)} %all-gather.3.cloned.1.call-done) | copy-start | bytes 3145732
  67.6 18.3 %copy-start.18 = (f32[1024]{0:T(1024)S(1)}, f32[1024]{0:T(1024)}, u32[]{:S(2)}) copy-start(f32[1024]{0:T(1024)} %convert_element_type.129) | copy-start | bytes 12292
  67.6 18.3 %copy-start.31 = (bf16[1024,128]{1,0:T(8,128)(2,1)S(1)}, bf16[1024,128]{1,0:T(8,128)(2,1)}, u32[]{:S(2)}) copy-start(bf16[1024,128]{1,0:T(8,128)(2,1)} %param.21) | copy-start | bytes 786436
  71.1 15.4 %copy-start.10 = (pred[512,512]{0,1:T(8,128)(4,1)S(1)}, pred[512,512]{0,1:T(8,128)(4,1)}, u32[]{:S(2)}) copy-start(pred[512,512]{0,1:T(8,128)(4,1)} %get-tuple-element.71) | copy-start | bytes 786436
  71.2 23.2 %copy-start.15 = (bf16[512,2,64]{0,2,1:T(8,128)(2,1)}, bf16[512,2,64]{0,2,1:T(8,128)(2,1)S(1)}, u32[]{:S(2)}) copy-start(bf16[512,2,64]{0,2,1:T(8,128)(2,1)S(1)} %maximum_convert_fusion) | copy-start | bytes 393220
  71.2 30.7 %collective-permute-start = (bf16[512,128]{0,1:T(8,128)(2,1)S(1)}, bf16[512,128]{0,1:T(8,128)(2,1)S(1)}, u32[]{:S(2)}, u32[]{:S(2)}) collective-permute-start(bf16[512,128]{0,1:T(8,128)(2,1)S(1)} %bitcast.264), channel_id=1, source_target_pairs={{0,8},{8,16},{16,24},{24,32},{32,40},{40,48},{48,56},{56,64},{64,7... | collective-permute-start | bytes 393224 | tf_op jit(solution)/shard_map/ppermute | solution.py:13
  72.5 15.6 %collective-permute-start.12 = (bf16[512,128]{0,1:T(8,128)(2,1)S(1)}, bf16[512,128]{0,1:T(8,128)(2,1)S(1)}, u32[]{:S(2)}, u32[]{:S(2)}) collective-permute-start(bf16[512,128]{0,1:T(8,128)(2,1)S(1)} %bitcast.265), channel_id=1, source_target_pairs={{0,40},{8,48},{16,56},{24,64},{32,72},{40,80},{48,88},{56,96},{64,... | collective-permute-start | bytes 393224 | tf_op jit(solution)/shard_map/ppermute | solution.py:13
  76.8 13.2 %collective-permute-start.9 = (bf16[512,128]{0,1:T(8,128)(2,1)S(1)}, bf16[512,128]{0,1:T(8,128)(2,1)S(1)}, u32[]{:S(2)}, u32[]{:S(2)}) collective-permute-start(bf16[512,128]{0,1:T(8,128)(2,1)S(1)} %bitcast.266), channel_id=1, source_target_pairs={{0,32},{8,40},{16,48},{24,56},{32,64},{40,72},{48,80},{56,88},{64,... | collective-permute-start | bytes 393224 | tf_op jit(solution)/shard_map/ppermute | solution.py:13
  80.2 14.2 %collective-permute-start.6 = (bf16[512,128]{0,1:T(8,128)(2,1)S(1)}, bf16[512,128]{0,1:T(8,128)(2,1)S(1)}, u32[]{:S(2)}, u32[]{:S(2)}) collective-permute-start(bf16[512,128]{0,1:T(8,128)(2,1)S(1)} %bitcast.267), channel_id=1, source_target_pairs={{0,24},{8,32},{16,40},{24,48},{32,56},{40,64},{48,72},{56,80},{64,... | collective-permute-start | bytes 393224 | tf_op jit(solution)/shard_map/ppermute | solution.py:13
  83.3 21.9 %collective-permute-start.3 = (bf16[512,128]{0,1:T(8,128)(2,1)S(1)}, bf16[512,128]{0,1:T(8,128)(2,1)S(1)}, u32[]{:S(2)}, u32[]{:S(2)}) collective-permute-start(bf16[512,128]{0,1:T(8,128)(2,1)S(1)} %bitcast.268), channel_id=1, source_target_pairs={{0,16},{8,24},{16,32},{24,40},{32,48},{40,56},{48,64},{56,72},{64,... | collective-permute-start | bytes 393224 | tf_op jit(solution)/shard_map/ppermute | solution.py:13
  86.5 1.0 copy-start.32
  88.1 8.1 %collective-permute-start.18 = (bf16[512,128]{0,1:T(8,128)(2,1)S(1)}, bf16[512,128]{0,1:T(8,128)(2,1)S(1)}, u32[]{:S(2)}, u32[]{:S(2)}) collective-permute-start(bf16[512,128]{0,1:T(8,128)(2,1)S(1)} %bitcast.269), channel_id=1, source_target_pairs={{0,56},{8,64},{16,72},{24,80},{32,88},{40,96},{48,104},{56,112},{6... | collective-permute-start | bytes 393224 | tf_op jit(solution)/shard_map/ppermute | solution.py:13
  89.9 10.1 %collective-permute-start.21 = (bf16[512,128]{0,1:T(8,128)(2,1)S(1)}, bf16[512,128]{0,1:T(8,128)(2,1)S(1)}, u32[]{:S(2)}, u32[]{:S(2)}) collective-permute-start(bf16[512,128]{0,1:T(8,128)(2,1)S(1)} %bitcast.270), channel_id=1, source_target_pairs={{0,64},{8,72},{16,80},{24,88},{32,96},{40,104},{48,112},{56,120},{... | collective-permute-start | bytes 393224 | tf_op jit(solution)/shard_map/ppermute | solution.py:13
  94.4 18.5 %collective-permute-start.15 = (bf16[512,128]{0,1:T(8,128)(2,1)S(1)}, bf16[512,128]{0,1:T(8,128)(2,1)S(1)}, u32[]{:S(2)}, u32[]{:S(2)}) collective-permute-start(bf16[512,128]{0,1:T(8,128)(2,1)S(1)} %bitcast.271), channel_id=1, source_target_pairs={{0,48},{8,56},{16,64},{24,72},{32,80},{40,88},{48,96},{56,104},{64... | collective-permute-start | bytes 393224 | tf_op jit(solution)/shard_map/ppermute | solution.py:13
  96.2 29.7 %collective-permute-start.5 = (bf16[512,128]{0,1:T(8,128)(2,1)S(1)}, bf16[512,128]{0,1:T(8,128)(2,1)S(1)}, u32[]{:S(2)}, u32[]{:S(2)}) collective-permute-start(bf16[512,128]{0,1:T(8,128)(2,1)S(1)} %convolution_convert_fusion.2), channel_id=1, source_target_pairs={{0,16},{8,24},{16,32},{24,40},{32,48},{40,56},{48,64},{56,72},{64,... | collective-permute-start | bytes 393224 | tf_op jit(solution)/shard_map/ppermute | solution.py:13
  99.6 4.6 %copy-start.7 = (pred[512,512]{0,1:T(8,128)(4,1)S(1)}, pred[512,512]{0,1:T(8,128)(4,1)}, u32[]{:S(2)}) copy-start(pred[512,512]{0,1:T(8,128)(4,1)} %get-tuple-element.70) | copy-start | bytes 786436
  99.6 4.6 %copy-start.11 = (pred[512,512]{0,1:T(8,128)(4,1)S(1)}, pred[512,512]{0,1:T(8,128)(4,1)}, u32[]{:S(2)}) copy-start(pred[512,512]{0,1:T(8,128)(4,1)} %get-tuple-element.60) | copy-start | bytes 786436
  100.1 28.8 %collective-permute-start.8 = (bf16[512,128]{0,1:T(8,128)(2,1)S(1)}, bf16[512,128]{0,1:T(8,128)(2,1)S(1)}, u32[]{:S(2)}, u32[]{:S(2)}) collective-permute-start(bf16[512,128]{0,1:T(8,128)(2,1)S(1)} %convolution_convert_fusion.2), channel_id=1, source_target_pairs={{0,24},{8,32},{16,40},{24,48},{32,56},{40,64},{48,72},{56,80},{64,... | collective-permute-start | bytes 393224 | tf_op jit(solution)/shard_map/ppermute | solution.py:13
  101.9 29.4 %collective-permute-start.11 = (bf16[512,128]{0,1:T(8,128)(2,1)S(1)}, bf16[512,128]{0,1:T(8,128)(2,1)S(1)}, u32[]{:S(2)}, u32[]{:S(2)}) collective-permute-start(bf16[512,128]{0,1:T(8,128)(2,1)S(1)} %convolution_convert_fusion.2), channel_id=1, source_target_pairs={{0,32},{8,40},{16,48},{24,56},{32,64},{40,72},{48,80},{56,88},{64,... | collective-permute-start | bytes 393224 | tf_op jit(solution)/shard_map/ppermute | solution.py:13
  104.2 4.4 %copy-start.4 = (pred[512,512]{0,1:T(8,128)(4,1)S(1)}, pred[512,512]{0,1:T(8,128)(4,1)}, u32[]{:S(2)}) copy-start(pred[512,512]{0,1:T(8,128)(4,1)} %get-tuple-element.54) | copy-start | bytes 786436
  104.2 4.4 %copy-start.5 = (pred[512,512]{0,1:T(8,128)(4,1)S(1)}, pred[512,512]{0,1:T(8,128)(4,1)}, u32[]{:S(2)}) copy-start(pred[512,512]{0,1:T(8,128)(4,1)} %get-tuple-element.53) | copy-start | bytes 786436
  104.2 4.4 %copy-start.8 = (pred[512,512]{0,1:T(8,128)(4,1)S(1)}, pred[512,512]{0,1:T(8,128)(4,1)}, u32[]{:S(2)}) copy-start(pred[512,512]{0,1:T(8,128)(4,1)} %get-tuple-element.65) | copy-start | bytes 786436
  104.2 4.4 %copy-start.9 = (pred[512,512]{0,1:T(8,128)(4,1)S(1)}, pred[512,512]{0,1:T(8,128)(4,1)}, u32[]{:S(2)}) copy-start(pred[512,512]{0,1:T(8,128)(4,1)} %get-tuple-element.64) | copy-start | bytes 786436
  104.3 4.4 %copy-start.12 = (pred[512,512]{0,1:T(8,128)(4,1)S(1)}, pred[512,512]{0,1:T(8,128)(4,1)}, u32[]{:S(2)}) copy-start(pred[512,512]{0,1:T(8,128)(4,1)} %get-tuple-element.58) | copy-start | bytes 786436
  104.3 4.4 %copy-start.13 = (pred[512,512]{0,1:T(8,128)(4,1)S(1)}, pred[512,512]{0,1:T(8,128)(4,1)}, u32[]{:S(2)}) copy-start(pred[512,512]{0,1:T(8,128)(4,1)} %get-tuple-element.59) | copy-start | bytes 786436
  105.3 28.5 %collective-permute-start.14 = (bf16[512,128]{0,1:T(8,128)(2,1)S(1)}, bf16[512,128]{0,1:T(8,128)(2,1)S(1)}, u32[]{:S(2)}, u32[]{:S(2)}) collective-permute-start(bf16[512,128]{0,1:T(8,128)(2,1)S(1)} %convolution_convert_fusion.2), channel_id=1, source_target_pairs={{0,40},{8,48},{16,56},{24,64},{32,72},{40,80},{48,88},{56,96},{64,... | collective-permute-start | bytes 393224 | tf_op jit(solution)/shard_map/ppermute | solution.py:13
  112.9 22.0 %collective-permute-start.17 = (bf16[512,128]{0,1:T(8,128)(2,1)S(1)}, bf16[512,128]{0,1:T(8,128)(2,1)S(1)}, u32[]{:S(2)}, u32[]{:S(2)}) collective-permute-start(bf16[512,128]{0,1:T(8,128)(2,1)S(1)} %convolution_convert_fusion.2), channel_id=1, source_target_pairs={{0,48},{8,56},{16,64},{24,72},{32,80},{40,88},{48,96},{56,104},{64... | collective-permute-start | bytes 393224 | tf_op jit(solution)/shard_map/ppermute | solution.py:13
  125.9 10.1 %collective-permute-start.20 = (bf16[512,128]{0,1:T(8,128)(2,1)S(1)}, bf16[512,128]{0,1:T(8,128)(2,1)S(1)}, u32[]{:S(2)}, u32[]{:S(2)}) collective-permute-start(bf16[512,128]{0,1:T(8,128)(2,1)S(1)} %convolution_convert_fusion.2), channel_id=1, source_target_pairs={{0,56},{8,64},{16,72},{24,80},{32,88},{40,96},{48,104},{56,112},{6... | collective-permute-start | bytes 393224 | tf_op jit(solution)/shard_map/ppermute | solution.py:13
  128.9 8.3 %collective-permute-start.23 = (bf16[512,128]{0,1:T(8,128)(2,1)S(1)}, bf16[512,128]{0,1:T(8,128)(2,1)S(1)}, u32[]{:S(2)}, u32[]{:S(2)}) collective-permute-start(bf16[512,128]{0,1:T(8,128)(2,1)S(1)} %convolution_convert_fusion.2), channel_id=1, source_target_pairs={{0,64},{8,72},{16,80},{24,88},{32,96},{40,104},{48,112},{56,120},{... | collective-permute-start | bytes 393224 | tf_op jit(solution)/shard_map/ppermute | solution.py:13
  131.3 8.1 %collective-permute-start.2 = (bf16[512,128]{0,1:T(8,128)(2,1)S(1)}, bf16[512,128]{0,1:T(8,128)(2,1)S(1)}, u32[]{:S(2)}, u32[]{:S(2)}) collective-permute-start(bf16[512,128]{0,1:T(8,128)(2,1)S(1)} %convolution_convert_fusion.2), channel_id=1, source_target_pairs={{0,8},{8,16},{16,24},{24,32},{32,40},{40,48},{48,56},{56,64},{64,7... | collective-permute-start | bytes 393224 | tf_op jit(solution)/shard_map/ppermute | solution.py:13
  139.3 1.2 copy-start.14
  140.6 72.5 %copy-start.6 = (bf16[512,128]{1,0:T(8,128)(2,1)S(1)}, bf16[512,128]{1,0:T(8,128)(2,1)}, u32[]{:S(2)}) copy-start(bf16[512,128]{1,0:T(8,128)(2,1)} %param.15) | copy-start | bytes 393220
  141.0 73.0 %copy-start.27 = (bf16[1024]{0:T(1024)(128)(2,1)S(1)}, bf16[1024]{0:T(1024)(128)(2,1)}, u32[]{:S(2)}) copy-start(bf16[1024]{0:T(1024)(128)(2,1)} %param.26) | copy-start | bytes 6148
  142.4 117.0 %all-gather.5.cloned.1.call-start = ((), (), s32[]{:S(2)}) async-start(), calls=%async_computation.4 | async-start | bytes 1179648 | tf_op jit(solution)/shard_map/all_gather | solution.py:157
  213.7 125.0 %reduce-scatter.12.cloned.1.call-start = ((), (), s32[]{:S(2)}) async-start(), calls=%async_computation.7 | async-start | bytes 1179648
  260.9 3.4 copy-start.3
  267.3 1.5 copy-start.25
  267.3 1.5 copy-start.30
  267.3 1.8 copy-start.28
  267.3 1.9 copy-start.16
  268.7 142.0 %reduce-scatter.8.cloned.1.call-start = ((), (), s32[]{:S(2)}) async-start(), calls=%async_computation.5 | async-start | bytes 5013504 | tf_op jit(solution)/shard_map/reduce_scatter | solution.py:172
  274.0 65.8 %copy-start.1 = (bf16[512,128]{1,0:T(8,128)(2,1)S(1)}, bf16[512,128]{1,0:T(8,128)(2,1)}, u32[]{:S(2)}) copy-start(bf16[512,128]{1,0:T(8,128)(2,1)} %add_convert_fusion.1) | copy-start | bytes 393220
Sparse Core Ops, SparseCore 0:
  22.0 45.5 all-gather.2
  142.5 69.4 reduce-scatter.9
  215.0 44.3 all-gather.4
  268.8 69.9 reduce-scatter.11
  341.1 69.6 reduce-scatter.7
where the time goes:
time: 420 us; the launch traced here: 419 us
  waiting for transfers between devices  277 us (66%)
  starting transfers between devices  62.1 us (15%)
  matrix products  37.1 us (9%)
  other arithmetic  21.3 us (5%)
  between operations  14.9 us (4%)
  local copies, waits for them, and re-layouts  7.15 us (2%)
    unnamed x7, waiting for transfers between devices  134 us
    reduce_scatter x1, waiting for transfers between devices, per_device(): lax.psum_scatter(jnp.dot(selector, pair_rows, preferred_element_type=jnp....  70.2 us
    ppermute x24, starting transfers between devices, passed_along(): lax.ppermute(value, axis, [(source, source + steps) for source in range(i...  61.6 us
    all_gather x1, waiting for transfers between devices, per_device(): residual_full = lax.all_gather(residual_local, 'tp', axis=1, tiled=True)  45.3 us
    all_gather x1, waiting for transfers between devices, per_device(): token_rows = lax.all_gather(tokens, 'tp', axis=1, tiled=True)  26.5 us
    dot_general x9, matrix products, attend(): jnp.einsum('qhd,khd->hqk', query_rows, piece_keys.reshape(piece_rows, loc...  13 us
    dot_general x9, matrix products, attend(): jnp.einsum('hqk,khd->hqd', weights.astype(jnp.bfloat16), piece_values.res...  9.46 us
  transfers between devices with their start and end apart: 29, of which 6 were waited for; matrix products, arithmetic and copies ran while one was open for 11% of the time, Pallas kernels for 0%

commit v1 on v0

v1 whole, which is shorter than its diff:
```python
import functools

import jax
import jax.numpy as jnp
from jax import lax
from jax.experimental import pallas as pl
from jax.experimental.pallas import tpu as pltpu
from jax.sharding import PartitionSpec as P

MESH = pl.DeviceIdType.MESH
F32 = jnp.float32
BF16 = jnp.bfloat16
NEG = -1e30

T = 512
LANES = 128
CH = 4
KX = 144
N_SEQ = 16
N_TP = 8
PAGE = 64
PAGES_DEV = 9
PAGES = 144
REQS = 4


class Gather:
    COUNT = 14

    def __init__(self, own, part, slot, ring, pair, to_next, to_prev, to_pair, sems, base):
        self.own, self.part, self.slot = own, part, slot
        self.ring, self.pair = ring, pair
        self.targets = {"next": to_next, "prev": to_prev, "pair": to_pair}
        self.send, self.recv = sems
        self.base = base
        self.sent = []

    def at(self, dr, flip):
        ring = lax.rem(self.ring + (dr + 4), 4)
        return self.slot(ring, 1 - self.pair if flip else self.pair)

    def push(self, k, source, place, which, target):
        copy = pltpu.make_async_remote_copy(
            src_ref=source,
            dst_ref=self.part(place, which),
            send_sem=self.send.at[self.base + k],
            recv_sem=self.recv.at[self.base + k],
            device_id=self.targets[target],
            device_id_type=MESH,
        )
        copy.start()
        self.sent.append(copy)

    def wait(self, k, dr, flip, which):
        ref = self.part(self.at(dr, flip), which)
        pltpu.make_async_remote_copy(
            src_ref=ref,
            dst_ref=ref,
            send_sem=self.send.at[self.base + k],
            recv_sem=self.recv.at[self.base + k],
            device_id=self.targets["pair"],
            device_id_type=MESH,
        ).wait_recv()

    def start(self):
        mine = self.at(0, False)
        for which in (0, 1):
            self.push(which, self.own(which), mine, which, "pair")
        for which in (0, 1):
            self.push(2 + which, self.own(which), mine, which, "next")
            self.push(5 - which, self.own(1 - which), mine, 1 - which, "prev")

    def relay_pair(self):
        place = self.at(0, True)
        self.wait(0, 0, True, 0)
        self.wait(1, 0, True, 1)
        for which in (0, 1):
            self.push(6 + which, self.part(place, which), place, which, "next")
            self.push(9 - which, self.part(place, 1 - which), place, 1 - which, "prev")

    def relay_ring(self, flip):
        first = 6 if flip else 2
        onward = 12 if flip else 10
        before, after = self.at(-1, flip), self.at(1, flip)
        self.wait(first, -1, flip, 0)
        self.push(onward, self.part(before, 0), before, 0, "next")
        self.wait(first + 3, 1, flip, 1)
        self.push(onward + 1, self.part(after, 1), after, 1, "prev")
        self.wait(first + 1, -1, flip, 1)
        self.wait(first + 2, 1, flip, 0)

    def finish(self, flip):
        onward = 12 if flip else 10
        self.wait(onward, 2, flip, 0)
        self.wait(onward + 1, 2, flip, 1)

    def drain(self):
        for copy in self.sent:
            copy.wait_send()


def spread(row):
    return jnp.broadcast_to(row, (LANES, LANES)).T


def kernel(
    lengths,
    page_table,
    var_bias,
    tokens,
    variate,
    positions,
    frequency,
    gain_attn,
    gain_ffn,
    w_query,
    w_key,
    w_value,
    w_out,
    w_gate,
    w_up,
    w_down,
    mixed,
    k_all,
    v_all,
    tok_buf,
    w_qkv,
    kbuf,
    vbuf,
    qbuf,
    peak,
    acc,
    wout_buf,
    att_own,
    att_buf,
    res_buf,
    normed_buf,
    gate_buf,
    up_buf,
    down_buf,
    part_buf,
    hop_buf,
    near_buf,
    sum_buf,
    pair_tx,
    pair_rx,
    table,
    send_sem,
    recv_sem,
    load_sem,
):
    sems = (send_sem, recv_sem)
    me = lax.axis_index("seq")
    tp = lax.axis_index("tp")
    y, xl, core = me // 4, lax.rem(me // 2, 2), lax.rem(me, 2)
    z, xh = tp // 2, lax.rem(tp, 2)

    def seq_of(ys, xs, cs):
        return ys * 4 + xs * 2 + cs

    tp_at = lambda t: {"seq": me, "tp": t}
    seq_at = lambda s: {"seq": s, "tp": tp}
    z_next, z_prev = lax.rem(z + 1, 4), lax.rem(z + 3, 4)
    y_next, y_prev = lax.rem(y + 1, 4), lax.rem(y + 3, 4)

    loads = [
        pltpu.make_async_copy(w_query, w_qkv.at[:, pl.ds(0, 128)], load_sem.at[0]),
        pltpu.make_async_copy(w_key, w_qkv.at[:, pl.ds(128, 128)], load_sem.at[1]),
        pltpu.make_async_copy(w_value, w_qkv.at[:, pl.ds(256, 128)], load_sem.at[2]),
        pltpu.make_async_copy(w_gate, gate_buf, load_sem.at[3]),
        pltpu.make_async_copy(w_up, up_buf, load_sem.at[4]),
        pltpu.make_async_copy(w_down, down_buf, load_sem.at[5]),
    ]
    for load in loads:
        load.start()

    barrier = pltpu.get_barrier_semaphore()
    peers = [tp_at(lax.rem(tp + d, N_TP)) for d in range(1, N_TP)]
    peers += [
        seq_at(seq_of(y, xl, 1 - core)),
        seq_at(seq_of(y, 1 - xl, core)),
        seq_at(seq_of(y_next, xl, core)),
        seq_at(seq_of(y_prev, xl, core)),
    ]
    for peer in peers:
        pl.semaphore_signal(barrier, inc=1, device_id=peer, device_id_type=MESH)
    pl.semaphore_wait(barrier, len(peers))

    tp_targets = (tp_at(z_next * 2 + xh), tp_at(z_prev * 2 + xh), tp_at(z * 2 + 1 - xh))
    tp_slot = lambda r, p: r * 2 + p

    tok = Gather(
        lambda w: tokens.at[pl.ds(w * 256, 256)],
        lambda s, w: tok_buf.at[s, pl.ds(w * 256, 256)],
        tp_slot, z, xh, *tp_targets, sems, 0,
    )
    tok.start()
    tok_buf[tp] = tokens[...]

    lane = lax.broadcasted_iota(jnp.int32, (LANES, LANES), 1)
    low = lax.rem(lane, 64) < 32
    for c in range(CH):
        angles = spread(positions[pl.ds(c, 1), :].astype(F32)) * frequency[...]
        rows = pl.ds(c * 128, 128)
        table[0, rows, :] = jnp.cos(angles)
        sine = jnp.sin(angles)
        table[1, rows, :] = jnp.where(low, -sine, sine)

    tok.relay_pair()
    tok.relay_ring(False)
    tok.relay_ring(True)
    tok.finish(False)
    tok.finish(True)
    for load in loads[:3]:
        load.wait()

    ends = []
    total = jnp.int32(0)
    for r in range(REQS):
        total = total + lengths[r]
        ends.append(total)
    gains = [gain_attn[:, pl.ds(t * 128, 128)].astype(F32) for t in range(N_TP)]

    def segments(index):
        count = jnp.zeros(index.shape, jnp.int32)
        for end in ends:
            count += jnp.where(index >= end, 1, 0)
        return count

    sub16 = lax.broadcasted_iota(jnp.int32, (16, LANES), 0)
    lane16 = lax.broadcasted_iota(jnp.int32, (16, LANES), 1)
    sub = lax.broadcasted_iota(jnp.int32, (LANES, LANES), 0)
    first_head = lane < 64

    def project(c, _):
        rows = pl.ds(pl.multiple_of(c * 128, 128), 128)
        blocks = [tok_buf[t, rows, :].astype(F32) for t in range(N_TP)]
        squares = blocks[0] * blocks[0]
        for block in blocks[1:]:
            squares += block * block
        scale = lax.rsqrt(jnp.sum(squares, axis=1, keepdims=True) * (1.0 / 1024) + 1e-6)
        normed = jnp.concatenate([(b * scale * g).astype(BF16) for b, g in zip(blocks, gains)], axis=1)
        out = jnp.dot(normed, w_qkv[...], preferred_element_type=F32)
        cosine, sine = table[0, rows, :], table[1, rows, :]

        def rope(u):
            partner = jnp.where(low, pltpu.roll(u, 96, 1), pltpu.roll(u, 32, 1))
            return (u * cosine + partner * sine).astype(BF16)

        query = rope(out[:, :128]).astype(F32) * 0.125
        keys = rope(out[:, 128:256])
        kbuf[me, c, pl.ds(0, 128), :] = keys.astype(F32).T.astype(BF16)
        vbuf[pl.ds(pl.multiple_of(me * T + c * 128, 128), 128), :] = out[:, 256:].astype(BF16)

        vrow = variate[pl.ds(c, 1), :]
        kseg = segments(me * T + c * 128 + lane16)
        vb = jnp.broadcast_to(vrow, (16, LANES))
        code = jnp.where(sub16 < 8, lax.rem(sub16, 4) - vb, kseg + 8 - sub16)
        kbuf[me, c, pl.ds(128, 16), :] = jnp.where(code == 0, 1.0, 0.0).astype(BF16)

        vcol = spread(vrow.astype(F32)).astype(jnp.int32)
        qseg = segments(me * T + c * 128 + sub)
        seg_part = jnp.where(qseg == lane - 8, 0.0, jnp.where(lane < 12, NEG, 0.0))
        for h in range(2):
            weight = jnp.where(vcol == lax.rem(lane, 4), var_bias[0, h], var_bias[1, h])
            head = weight.astype(BF16).astype(F32)
            extra = jnp.where(lane < 4, head, jnp.where(lane < 8, weight - head, seg_part))
            own = first_head if h == 0 else jnp.logical_not(first_head)
            place = pl.ds(pl.multiple_of(h * T + c * 128, 128), 128)
            qbuf[place, pl.ds(0, 128)] = jnp.where(own, query, 0.0).astype(BF16)
            qbuf[place, pl.ds(128, 16)] = extra[:, :16].astype(BF16)
        return 0

    lax.fori_loop(0, CH, project, 0)

    def kv_part(s, w):
        return kbuf.at[s] if w == 0 else vbuf.at[pl.ds(pl.multiple_of(s * T, T), T)]

    kv = Gather(
        lambda w: kv_part(me, w), kv_part,
        lambda r, p: seq_of(r, p, core), y, xl,
        seq_at(seq_of(y_next, xl, core)), seq_at(seq_of(y_prev, xl, core)), seq_at(seq_of(y, 1 - xl, core)),
        sems, 14,
    )
    core_base = 28
    core_sent = []

    def core_copy(k, s, w):
        ref = kv_part(s, w)
        return pltpu.make_async_remote_copy(
            src_ref=ref, dst_ref=ref,
            send_sem=send_sem.at[core_base + k], recv_sem=recv_sem.at[core_base + k],
            device_id=seq_at(seq_of(y, xl, 1 - core)), device_id_type=MESH,
        )

    order = [(0, False), (0, True), (-1, False), (1, False), (-1, True), (1, True), (2, False), (2, True)]

    def place_of(dr, flip, cs):
        return seq_of(lax.rem(y + dr + 4, 4), (1 - xl) if flip else xl, cs)

    def core_send(n):
        s = place_of(*order[n], core)
        for w in (0, 1):
            copy = core_copy(n * 2 + w, s, w)
            copy.start()
            core_sent.append(copy)

    def core_wait(n):
        s = place_of(*order[n], 1 - core)
        for w in (0, 1):
            core_copy(n * 2 + w, s, w).wait_recv()

    core_send(0)
    kv.start()

    wo = Gather(
        lambda w: w_out.at[pl.ds(w * 64, 64)],
        lambda s, w: wout_buf.at[s, pl.ds(w * 64, 64)],
        tp_slot, z, xh, *tp_targets, sems, 44,
    )
    wo.start()
    wout_buf[tp] = w_out[...]

    ones = jnp.ones((T, LANES), BF16)

    def attend(s, diagonal):
        keys = jnp.concatenate([kbuf[s, c] for c in range(CH)], axis=1)
        values = jnp.concatenate([vbuf[pl.ds(pl.multiple_of(s * T, T), T), :], ones], axis=1)

        def tile(i, _):
            for h in range(2):
                rows = pl.ds(pl.multiple_of(h * T + i * 128, 128), 128)
                score = jnp.dot(qbuf[rows, :], keys, preferred_element_type=F32)
                if diagonal:
                    qi = i * 128 + lax.broadcasted_iota(jnp.int32, (128, T), 0)
                    ki = lax.broadcasted_iota(jnp.int32, (128, T), 1)
                    score = jnp.where(ki <= qi, score, NEG)
                    top = jnp.broadcast_to(jnp.max(score, axis=1, keepdims=True), (128, LANES))
                else:
                    before = peak[rows, :]
                    top = jnp.maximum(before, jnp.max(score, axis=1, keepdims=True))
                weight = jnp.exp(score - jnp.concatenate([top] * CH, axis=1)).astype(BF16)
                product = jnp.dot(weight, values, preferred_element_type=F32)
                if not diagonal:
                    fade = jnp.exp(before - top)
                    product += acc[rows, :] * jnp.concatenate([fade, fade], axis=1)
                acc[rows, :] = product
                peak[rows, :] = top
            return 0

        lax.fori_loop(0, CH, tile, 0)

    def attend_if(n, cs):
        s = place_of(*order[n], cs)

        @pl.when(jnp.logical_and(s < me, s >= me - 8))
        def _():
            attend(s, False)

    attend(me, True)
    core_wait(0)
    attend_if(0, 1 - core)
    kv.relay_pair()
    core_send(1)
    kv.relay_ring(False)
    core_send(2)
    core_send(3)
    wo.relay_pair()
    attend_if(1, core)
    attend_if(2, core)
    core_wait(1)
    core_wait(2)
    core_wait(3)
    wo.relay_ring(False)
    attend_if(1, 1 - core)
    attend_if(2, 1 - core)
    kv.relay_ring(True)
    core_send(4)
    core_send(5)
    wo.relay_ring(True)
    attend_if(4, core)
    kv.finish(False)
    core_send(6)
    core_wait(4)
    core_wait(5)
    attend_if(4, 1 - core)
    attend_if(6, core)
    kv.finish(True)
    core_send(7)
    core_wait(6)
    attend_if(6, 1 - core)
    attend_if(7, core)
    core_wait(7)
    attend_if(7, 1 - core)

    stores = [
        pltpu.make_async_copy(kbuf, k_all, load_sem.at[6]),
        pltpu.make_async_copy(vbuf, v_all, load_sem.at[7]),
    ]
    for store in stores:
        store.start()

    for c in range(CH):
        low_rows, high_rows = pl.ds(c * 128, 128), pl.ds(T + c * 128, 128)
        a, b = acc[low_rows, :], acc[high_rows, :]
        att = jnp.where(first_head, a[:, :128] / a[:, 128:], b[:, :128] / b[:, 128:]).astype(BF16)
        att_own[pl.ds(2 * c, 2)] = att.reshape(2, 64, 128)
    swap_base = 58
    swaps = []

    def swap(d, target, source_slot, place):
        return pltpu.make_async_remote_copy(
            src_ref=att_own.at[source_slot], dst_ref=att_buf.at[place],
            send_sem=send_sem.at[swap_base + d], recv_sem=recv_sem.at[swap_base + d],
            device_id=tp_at(target), device_id_type=MESH,
        )

    for d in (4, 3, 5, 2, 6, 1, 7):
        target = lax.rem(tp + d, N_TP)
        copy = swap(d, target, target, tp)
        copy.start()
        swaps.append(copy)
    att_buf[tp] = att_own[tp]
    wo.finish(False)
    wo.finish(True)
    for d in range(1, N_TP):
        origin = lax.rem(tp - d + N_TP, N_TP)
        swap(d, origin, origin, origin).wait_recv()
    rows_att = jnp.concatenate([att_buf[t] for t in range(N_TP)], axis=1)
    projected = jnp.dot(rows_att, wout_buf[...].reshape(1024, 1024), preferred_element_type=F32)
    own_rows = pl.ds(pl.multiple_of(tp * 64, 64), 64)
    own_tokens = jnp.concatenate([tok_buf[t, own_rows, :] for t in range(N_TP)], axis=1)
    res_buf[tp] = (own_tokens.astype(F32) + projected).astype(BF16)

    res = Gather(
        lambda w: res_buf.at[tp, pl.ds(w * 32, 32)],
        lambda s, w: res_buf.at[s, pl.ds(w * 32, 32)],
        tp_slot, z, xh, *tp_targets, sems, 66,
    )
    res.start()
    res.relay_pair()
    res.relay_ring(False)
    res.relay_ring(True)
    res.finish(False)
    res.finish(True)
    for load in loads[3:]:
        load.wait()

    def normalise(s, _):
        x = res_buf[s].astype(F32)
        scale = lax.rsqrt(jnp.sum(x * x, axis=1, keepdims=True) * (1.0 / 1024) + 1e-6)
        normed_buf[pl.ds(pl.multiple_of(s * 64, 64), 64), :] = (x * scale * gain_ffn[...].astype(F32)).astype(BF16)
        return 0

    lax.fori_loop(0, N_TP, normalise, 0)

    ring_base = 80
    ring_sent = []

    def ring_copy(k, source, place, target):
        return pltpu.make_async_remote_copy(
            src_ref=source, dst_ref=place,
            send_sem=send_sem.at[ring_base + k], recv_sem=recv_sem.at[ring_base + k],
            device_id=target, device_id_type=MESH,
        )

    def ring_start(k, source, place, target):
        copy = ring_copy(k, source, place, target)
        copy.start()
        ring_sent.append(copy)

    z_far = lax.rem(z + 2, 4)
    next_at, prev_at, pair_at = tp_targets

    def pieces(zs, j, half):
        return part_buf.at[pl.ds(zs * 2, 2), pl.ds(j * 256 + half * 128, 128)]

    def ffn(j):
        rows = pl.ds(j * 256, 256)
        x = normed_buf[rows, :]
        gate = jnp.dot(x, gate_buf[...], preferred_element_type=F32)
        up = jnp.dot(x, up_buf[...], preferred_element_type=F32)
        hidden = (gate * (1.0 / (1.0 + jnp.exp(-gate))) * up).astype(BF16)
        for t in range(N_TP):
            part_buf[t, rows, :] = jnp.dot(
                hidden, down_buf[:, pl.ds(t * 128, 128)], preferred_element_type=F32
            ).astype(BF16)

    def ring_first(j):
        k = j * 8
        ring_start(k, pieces(z_far, j, 0), hop_buf.at[j, 0], next_at)
        ring_start(k + 1, pieces(z_far, j, 1), hop_buf.at[j, 1], prev_at)
        ring_start(k + 2, pieces(z_next, j, 1), near_buf.at[j, 0, 1], next_at)
        ring_start(k + 3, pieces(z_prev, j, 0), near_buf.at[j, 1, 0], prev_at)

    def ring_second(j):
        k = j * 8
        ring_copy(k, hop_buf.at[j, 0], hop_buf.at[j, 0], next_at).wait_recv()
        sum_buf[j, 0] = (hop_buf[j, 0].astype(F32) + pieces(z_next, j, 0)[...].astype(F32)).astype(BF16)
        ring_start(k + 4, sum_buf.at[j, 0], near_buf.at[j, 0, 0], next_at)
        ring_copy(k + 1, hop_buf.at[j, 1], hop_buf.at[j, 1], prev_at).wait_recv()
        sum_buf[j, 1] = (hop_buf[j, 1].astype(F32) + pieces(z_prev, j, 1)[...].astype(F32)).astype(BF16)
        ring_start(k + 5, sum_buf.at[j, 1], near_buf.at[j, 1, 1], prev_at)

    def own_sum(j, xs):
        total = []
        for half in (0, 1):
            own = part_buf[z * 2 + xs, pl.ds(j * 256 + half * 128, 128), :].astype(F32)
            total.append(own + near_buf[j, 0, half, xs].astype(F32) + near_buf[j, 1, half, xs].astype(F32))
        return jnp.concatenate(total, axis=0)

    def ring_third(j):
        k = j * 8
        ring_copy(k + 2, near_buf.at[j, 0, 1], near_buf.at[j, 0, 1], next_at).wait_recv()
        ring_copy(k + 3, near_buf.at[j, 1, 0], near_buf.at[j, 1, 0], prev_at).wait_recv()
        ring_copy(k + 4, near_buf.at[j, 0, 0], near_buf.at[j, 0, 0], next_at).wait_recv()
        ring_copy(k + 5, near_buf.at[j, 1, 1], near_buf.at[j, 1, 1], prev_at).wait_recv()
        pair_tx[j] = own_sum(j, 1 - xh).astype(BF16)
        ring_start(k + 6, pair_tx.at[j], pair_rx.at[j], pair_at)

    def ring_last(j):
        ring_copy(j * 8 + 6, pair_rx.at[j], pair_rx.at[j], pair_at).wait_recv()
        columns = pl.ds(pl.multiple_of(tp * 128, 128), 128)
        kept = jnp.concatenate([res_buf[4 * j + i, :, columns] for i in range(4)], axis=0).astype(F32)
        mixed[pl.ds(j * 256, 256), :] = (kept + own_sum(j, xh) + pair_rx[j].astype(F32)).astype(BF16)

    ffn(0)
    ring_first(0)
    ffn(1)
    ring_first(1)

    ring_second(0)
    ring_second(1)
    ring_third(0)
    ring_third(1)
    ring_last(0)
    ring_last(1)
    for gather in (tok, kv, wo, res):
        gather.drain()
    for copy in core_sent + swaps + ring_sent:
        copy.wait_send()
    for store in stores:
        store.wait()


def cache_kernel(lengths, page_table, k_all, v_all, cache, k_win, v_win, sem):
    me = lax.axis_index("seq")

    def find(l, found):
        page = page_table[l]
        return tuple(jnp.where(page == me * PAGES_DEV + p, l, f) for p, f in enumerate(found))

    found = lax.fori_loop(0, PAGES, find, (jnp.int32(-1),) * PAGES_DEV)
    starts, bases = [], []
    begin, base = jnp.int32(0), jnp.int32(0)
    for r in range(REQS):
        starts.append(begin)
        bases.append(base)
        begin = begin + lengths[r]
        base = base + (lengths[r] + PAGE - 1) // PAGE
    plans = []
    for p in range(PAGES_DEV):
        l = found[p]
        first, size = jnp.int32(0), jnp.int32(0)
        for r in range(REQS):
            offset = (l - bases[r]) * PAGE
            inside = jnp.logical_and(l >= bases[r], offset < lengths[r])
            first = jnp.where(inside, starts[r] + offset, first)
            size = jnp.where(inside, jnp.minimum(lengths[r] - offset, PAGE), size)
        window = jnp.minimum(first // 16 * 16, N_SEQ * T - 80)
        chunk = jnp.minimum(first // 128, N_SEQ * CH - 2)
        copies = [
            pltpu.make_async_copy(v_all.at[pl.ds(pl.multiple_of(window, 16), 80)], v_win.at[p], sem.at[p, 0]),
            pltpu.make_async_copy(k_all.at[pl.ds(chunk, 2)], k_win.at[p], sem.at[p, 1]),
        ]
        for copy in copies:
            copy.start()
        plans.append((first - window, first - chunk * 128, size, copies))
    sel_row = lax.broadcasted_iota(jnp.int32, (PAGE, 80), 0)
    sel_col = lax.broadcasted_iota(jnp.int32, (PAGE, 80), 1)
    key_row = lax.broadcasted_iota(jnp.int32, (PAGE, 256), 0)
    key_col = lax.broadcasted_iota(jnp.int32, (PAGE, 256), 1)
    for p, (v_shift, k_shift, size, copies) in enumerate(plans):
        for copy in copies:
            copy.wait()
        picked = jnp.logical_and(sel_col == sel_row + v_shift, sel_row < size)
        values = jnp.dot(jnp.where(picked, 1.0, 0.0).astype(BF16), v_win[p], preferred_element_type=F32)
        chosen = jnp.logical_and(key_col == key_row + k_shift, key_row < size)
        keys = jnp.concatenate([k_win[p, 0, pl.ds(0, 128), :], k_win[p, 1, pl.ds(0, 128), :]], axis=1)
        rows = lax.dot_general(
            jnp.where(chosen, 1.0, 0.0).astype(BF16), keys,
            (((1,), (1,)), ((), ())), preferred_element_type=F32,
        )
        cache[pl.ds(p * PAGE, PAGE)] = jnp.stack([rows, values], axis=1).astype(BF16)


N_SEMS = 96


def per_device(
    tokens, variate, positions, lengths, page_table, gain_attn, w_query, w_key, w_value, var_bias,
    w_out, gain_ffn, w_gate, w_up, w_down,
):
    half = jnp.arange(LANES, dtype=jnp.int32) % 32
    frequency = (10000.0 ** (-(half.astype(F32)) / 32.0)).reshape(1, LANES)
    vmem = pl.BlockSpec(memory_space=pltpu.VMEM)
    smem = pl.BlockSpec(memory_space=pltpu.SMEM)
    anywhere = pl.BlockSpec(memory_space=pl.ANY)
    buf = lambda *shape: pltpu.VMEM(shape, BF16)
    mixed, k_all, v_all = pl.pallas_call(
        kernel,
        out_shape=(
            jax.ShapeDtypeStruct((T, LANES), BF16),
            jax.ShapeDtypeStruct((N_SEQ, CH, KX, LANES), BF16),
            jax.ShapeDtypeStruct((N_SEQ * T, LANES), BF16),
        ),
        in_specs=[smem] * 3 + [vmem] * 6 + [anywhere] * 3 + [vmem] + [anywhere] * 3,
        out_specs=(vmem, anywhere, anywhere),
        scratch_shapes=[
            buf(N_TP, T, LANES),
            buf(1024, 384),
            buf(N_SEQ, CH, KX, LANES),
            buf(N_SEQ * T, LANES),
            buf(2 * T, KX),
            pltpu.VMEM((2 * T, LANES), F32),
            pltpu.VMEM((2 * T, 2 * LANES), F32),
            buf(N_TP, LANES, 1024),
            buf(N_TP, 64, LANES),
            buf(N_TP, 64, LANES),
            buf(N_TP, 64, 1024),
            buf(T, 1024),
            buf(1024, T),
            buf(1024, T),
            buf(T, 1024),
            buf(N_TP, T, LANES),
            buf(2, 2, 2, 128, LANES),
            buf(2, 2, 2, 2, 128, LANES),
            buf(2, 2, 2, 128, LANES),
            buf(2, 256, LANES),
            buf(2, 256, LANES),
            pltpu.VMEM((2, T, LANES), F32),
            pltpu.SemaphoreType.DMA((N_SEMS,)),
            pltpu.SemaphoreType.DMA((N_SEMS,)),
            pltpu.SemaphoreType.DMA((8,)),
        ],
        compiler_params=pltpu.CompilerParams(collective_id=0, has_side_effects=True),
        name="layer",
    )(
        lengths, page_table, var_bias, tokens, variate.reshape(CH, LANES), positions.reshape(CH, LANES), frequency,
        gain_attn.reshape(1, 1024), gain_ffn.reshape(1, 1024), w_query, w_key, w_value, w_out, w_gate, w_up, w_down,
    )
    cache = pl.pallas_call(
        cache_kernel,
        out_shape=jax.ShapeDtypeStruct((PAGES_DEV * PAGE, 2, LANES), BF16),
        in_specs=[smem] * 2 + [anywhere] * 2,
        out_specs=vmem,
        scratch_shapes=[
            buf(PAGES_DEV, 2, KX, LANES),
            buf(PAGES_DEV, 80, LANES),
            pltpu.SemaphoreType.DMA((PAGES_DEV, 2)),
        ],
        name="pages",
    )(lengths, page_table, k_all.reshape(N_SEQ * CH, KX, LANES), v_all)
    return mixed, cache


def solution(mesh):
    placed = (
        P("seq", "tp"), P("seq"), P("seq"), P(), P(), P(), P(None, "tp"), P(None, "tp"), P(None, "tp"),
        P(None, "tp"), P("tp", None), P(), P(None, "tp"), P(None, "tp"), P("tp", None),
    )
    return jax.shard_map(
        per_device,
        mesh=mesh,
        in_specs=placed,
        out_specs=(P("seq", "tp"), P("seq", None, "tp")),
        check_vma=False,
    )
```

time: 420 us -> 106 us (0.25)
  the two profiles are of different devices: /device:TPU:0 before, /device:TPU:48 now
where the time goes in v1:
time: 106 us; the launch traced here: 105 us
  Pallas kernels  101 us (95%)
  local copies, waits for them, and re-layouts  3.22 us (3%)
    pallas_call x1, Pallas kernels, per_device(): pl.pallas_call(kernel, out_shape=(jax.ShapeDtypeStruct((T, LANES), BF16),...  94 us
    pallas_call x1, Pallas kernels, per_device(): pl.pallas_call(cache_kernel, out_shape=jax.ShapeDtypeStruct((PAGES_DEV *...  7.03 us

profile of v1, /device:TPU:48, one launch (start us, length us, event | category | flops | bytes accessed | tf_op | source)
XLA Modules:
  0.0 105.4 jit_solution(13871110820077358979)
XLA Ops:
  0.6 0.5 fusion.3.frequency
  1.2 1.3 %reshape.56.gain_attn = bf16[1,1024]{1,0:T(2,128)(2,1)} reshape(bf16[1024]{0:T(1024)(128)(2,1)} %param.20) | data formatting | bytes 4096 | tf_op jit(solution)/shard_map/reshape | solution.py:650
  2.4 1.3 %reshape.57.gain_ffn = bf16[1,1024]{1,0:T(2,128)(2,1)} reshape(bf16[1024]{0:T(1024)(128)(2,1)} %param.26) | data formatting | bytes 4096 | tf_op jit(solution)/shard_map/reshape | solution.py:650
  3.7 94.0 %layer.1 = (bf16[512,128]{1,0:T(8,128)(2,1)}, bf16[16,4,144,128]{3,2,1,0:T(8,128)(2,1)}, bf16[8192,128]{1,0:T(8,128)(2,1)}) custom-call(s32[4]{0:T(128)} %lengths.3, s32[144]{0:T(256)} %page_table.3, f32[2,2]{1,0:T(2,128)} %var_bias.1, bf16[512,128]{1,0:T(8,128)(2,1)} %tokens.1, s32[4,128]{1,0:T(4,128)} %bitcast.4, s32[4,128]{1,0:T(4,128)} %bitcast.5, ...), custom_call_target="tpu_custom_call" | custom-call | tf_op jit(solution)/shard_map/layer/pallas_call | solution.py:610
  97.7 0.0 copy-start
  97.7 7.0 %pages.1 = bf16[576,2,128]{2,1,0:T(2,128)(2,1)} custom-call(s32[4]{0:T(128)} %lengths.3, s32[144]{0:T(256)} %page_table.3, bf16[64,144,128]{2,1,0:T(8,128)(2,1)} %bitcast.3, bf16[8192,128]{1,0:T(8,128)(2,1)} %get-tuple-element.7.v_all), custom_call_target="tpu_custom_call" | custom-call | tf_op jit(solution)/shard_map/pages/pallas_call | solution.py:652
  104.7 0.0 copy-done
  104.7 0.7 copy.18
Async XLA Ops:
  97.7 7.0 %copy-start = (bf16[512,128]{1,0:T(8,128)(2,1)S(1)}, bf16[512,128]{1,0:T(8,128)(2,1)}, u32[]{:S(2)}) copy-start(bf16[512,128]{1,0:T(8,128)(2,1)} %get-tuple-element.10) | copy-start | bytes 393220

commit v2 on v1

--- a/solution.py
+++ b/solution.py
@@ -1,4 +1,4 @@
-import functools
+import math
 
 import jax
 import jax.numpy as jnp
@@ -72,11 +72,10 @@
 
     def relay_pair(self):
         place = self.at(0, True)
-        self.wait(0, 0, True, 0)
-        self.wait(1, 0, True, 1)
         for which in (0, 1):
+            self.wait(which, 0, True, which)
             self.push(6 + which, self.part(place, which), place, which, "next")
-            self.push(9 - which, self.part(place, 1 - which), place, 1 - which, "prev")
+            self.push(8 + which, self.part(place, which), place, which, "prev")
 
     def relay_ring(self, flip):
         first = 6 if flip else 2
@@ -110,7 +109,6 @@
     tokens,
     variate,
     positions,
-    frequency,
     gain_attn,
     gain_ffn,
     w_query,
@@ -199,15 +197,16 @@
 
     lane = lax.broadcasted_iota(jnp.int32, (LANES, LANES), 1)
     low = lax.rem(lane, 64) < 32
+    frequency = jnp.exp(lax.rem(lane, 32).astype(F32) * (-math.log(10000.0) / 32.0))
     for c in range(CH):
-        angles = spread(positions[pl.ds(c, 1), :].astype(F32)) * frequency[...]
+        angles = spread(positions[pl.ds(c, 1), :].astype(F32)) * frequency
         rows = pl.ds(c * 128, 128)
         table[0, rows, :] = jnp.cos(angles)
         sine = jnp.sin(angles)
         table[1, rows, :] = jnp.where(low, -sine, sine)
 
+    tok.relay_ring(False)
     tok.relay_pair()
-    tok.relay_ring(False)
     tok.relay_ring(True)
     tok.finish(False)
     tok.finish(True)
@@ -219,7 +218,7 @@
     for r in range(REQS):
         total = total + lengths[r]
         ends.append(total)
-    gains = [gain_attn[:, pl.ds(t * 128, 128)].astype(F32) for t in range(N_TP)]
+    gains = [gain_attn[pl.ds(t, 1), :].astype(F32) for t in range(N_TP)]
 
     def segments(index):
         count = jnp.zeros(index.shape, jnp.int32)
@@ -348,7 +347,7 @@
                 peak[rows, :] = top
             return 0
 
-        lax.fori_loop(0, CH, tile, 0)
+        lax.fori_loop(0, CH, tile, 0, unroll=2)
 
     def attend_if(n, cs):
         s = place_of(*order[n], cs)
@@ -438,18 +437,20 @@
         tp_slot, z, xh, *tp_targets, sems, 66,
     )
     res.start()
+    res.relay_ring(False)
     res.relay_pair()
-    res.relay_ring(False)
     res.relay_ring(True)
     res.finish(False)
     res.finish(True)
     for load in loads[3:]:
         load.wait()
 
+    ffn_gain = jnp.concatenate([gain_ffn[pl.ds(t, 1), :].astype(F32) for t in range(N_TP)], axis=1)
+
     def normalise(s, _):
         x = res_buf[s].astype(F32)
         scale = lax.rsqrt(jnp.sum(x * x, axis=1, keepdims=True) * (1.0 / 1024) + 1e-6)
-        normed_buf[pl.ds(pl.multiple_of(s * 64, 64), 64), :] = (x * scale * gain_ffn[...].astype(F32)).astype(BF16)
+        normed_buf[pl.ds(pl.multiple_of(s * 64, 64), 64), :] = (x * scale * ffn_gain).astype(BF16)
         return 0
 
     lax.fori_loop(0, N_TP, normalise, 0)
@@ -601,8 +602,6 @@
     tokens, variate, positions, lengths, page_table, gain_attn, w_query, w_key, w_value, var_bias,
     w_out, gain_ffn, w_gate, w_up, w_down,
 ):
-    half = jnp.arange(LANES, dtype=jnp.int32) % 32
-    frequency = (10000.0 ** (-(half.astype(F32)) / 32.0)).reshape(1, LANES)
     vmem = pl.BlockSpec(memory_space=pltpu.VMEM)
     smem = pl.BlockSpec(memory_space=pltpu.SMEM)
     anywhere = pl.BlockSpec(memory_space=pl.ANY)
@@ -614,7 +613,7 @@
             jax.ShapeDtypeStruct((N_SEQ, CH, KX, LANES), BF16),
             jax.ShapeDtypeStruct((N_SEQ * T, LANES), BF16),
         ),
-        in_specs=[smem] * 3 + [vmem] * 6 + [anywhere] * 3 + [vmem] + [anywhere] * 3,
+        in_specs=[smem] * 3 + [vmem] * 5 + [anywhere] * 3 + [vmem] + [anywhere] * 3,
         out_specs=(vmem, anywhere, anywhere),
         scratch_shapes=[
             buf(N_TP, T, LANES),
@@ -646,8 +645,8 @@
         compiler_params=pltpu.CompilerParams(collective_id=0, has_side_effects=True),
         name="layer",
     )(
-        lengths, page_table, var_bias, tokens, variate.reshape(CH, LANES), positions.reshape(CH, LANES), frequency,
-        gain_attn.reshape(1, 1024), gain_ffn.reshape(1, 1024), w_query, w_key, w_value, w_out, w_gate, w_up, w_down,
+        lengths, page_table, var_bias, tokens, variate.reshape(CH, LANES), positions.reshape(CH, LANES),
+        gain_attn.reshape(N_TP, LANES), gain_ffn.reshape(N_TP, LANES), w_query, w_key, w_value, w_out, w_gate, w_up, w_down,
     )
     cache = pl.pallas_call(
         cache_kernel,

time: 106 us -> 98.2 us (0.926); the launches traced: 105 us -> 96.3 us
  Pallas kernels: 101 us -> 94.9 us
  local copies, waits for them, and re-layouts: 3.22 us -> 0.66 us
    pallas_call x1, Pallas kernels: 94 us -> 87.9 us  [per_device(): pl.pallas_call(kernel, out_shape=(jax.ShapeDtypeStruct((T, LANES), BF16),...]
    reshape x2 -> x0, local copies, waits for them, and re-layouts: 2.55 us -> none  [the longest x1 1.28 us: per_device(): gain_attn.reshape(1, 1024)]
where the time goes in v2:
time: 98.2 us; the launch traced here: 96.3 us
  Pallas kernels  94.9 us (97%)
    pallas_call x1, Pallas kernels, per_device(): pl.pallas_call(kernel, out_shape=(jax.ShapeDtypeStruct((T, LANES), BF16),...  87.9 us
    pallas_call x1, Pallas kernels, per_device(): pl.pallas_call(cache_kernel, out_shape=jax.ShapeDtypeStruct((PAGES_DEV *...  7.03 us

profile of v2, /device:TPU:48, one launch (start us, length us, event | category | flops | bytes accessed | tf_op | source)
XLA Modules:
  0.0 96.3 jit_solution(15477364775773154909)
XLA Ops:
  0.6 87.9 %layer.1 = (bf16[512,128]{1,0:T(8,128)(2,1)}, bf16[16,4,144,128]{3,2,1,0:T(8,128)(2,1)}, bf16[8192,128]{1,0:T(8,128)(2,1)}) custom-call(s32[4]{0:T(128)} %lengths.3, s32[144]{0:T(256)} %page_table.3, f32[2,2]{1,0:T(2,128)} %var_bias.1, bf16[512,128]{1,0:T(8,128)(2,1)} %tokens.1, s32[4,128]{1,0:T(4,128)} %bitcast.6, s32[4,128]{1,0:T(4,128)} %bitcast.7, ...), custom_call_target="tpu_custom_call" | custom-call | tf_op jit(solution)/shard_map/layer/pallas_call | solution.py:609
  88.6 0.0 copy-start
  88.6 7.0 %pages.1 = bf16[576,2,128]{2,1,0:T(2,128)(2,1)} custom-call(s32[4]{0:T(128)} %lengths.3, s32[144]{0:T(256)} %page_table.3, bf16[64,144,128]{2,1,0:T(8,128)(2,1)} %bitcast.5, bf16[8192,128]{1,0:T(8,128)(2,1)} %get-tuple-element.7.v_all), custom_call_target="tpu_custom_call" | custom-call | tf_op jit(solution)/shard_map/pages/pallas_call | solution.py:651
  95.6 0.0 copy-done
  95.6 0.7 copy.18
Async XLA Ops:
  88.6 7.0 %copy-start = (bf16[512,128]{1,0:T(8,128)(2,1)S(1)}, bf16[512,128]{1,0:T(8,128)(2,1)}, u32[]{:S(2)}) copy-start(bf16[512,128]{1,0:T(8,128)(2,1)} %get-tuple-element.10) | copy-start | bytes 393220

commit v3 on v2

--- a/solution.py
+++ b/solution.py
@@ -129,7 +129,6 @@
     peak,
     acc,
     wout_buf,
-    att_own,
     att_buf,
     res_buf,
     normed_buf,
@@ -402,58 +401,37 @@
     for c in range(CH):
         low_rows, high_rows = pl.ds(c * 128, 128), pl.ds(T + c * 128, 128)
         a, b = acc[low_rows, :], acc[high_rows, :]
-        att = jnp.where(first_head, a[:, :128] / a[:, 128:], b[:, :128] / b[:, 128:]).astype(BF16)
-        att_own[pl.ds(2 * c, 2)] = att.reshape(2, 64, 128)
-    swap_base = 58
-    swaps = []
-
-    def swap(d, target, source_slot, place):
-        return pltpu.make_async_remote_copy(
-            src_ref=att_own.at[source_slot], dst_ref=att_buf.at[place],
-            send_sem=send_sem.at[swap_base + d], recv_sem=recv_sem.at[swap_base + d],
-            device_id=tp_at(target), device_id_type=MESH,
-        )
-
-    for d in (4, 3, 5, 2, 6, 1, 7):
-        target = lax.rem(tp + d, N_TP)
-        copy = swap(d, target, target, tp)
-        copy.start()
-        swaps.append(copy)
-    att_buf[tp] = att_own[tp]
+        att_buf[tp, pl.ds(c * 128, 128), :] = jnp.where(
+            first_head, a[:, :128] / a[:, 128:], b[:, :128] / b[:, 128:]
+        ).astype(BF16)
+    att = Gather(
+        lambda w: att_buf.at[tp, pl.ds(w * 256, 256)],
+        lambda s, w: att_buf.at[s, pl.ds(w * 256, 256)],
+        tp_slot, z, xh, *tp_targets, sems, 66,
+    )
+    att.start()
     wo.finish(False)
     wo.finish(True)
-    for d in range(1, N_TP):
-        origin = lax.rem(tp - d + N_TP, N_TP)
-        swap(d, origin, origin, origin).wait_recv()
-    rows_att = jnp.concatenate([att_buf[t] for t in range(N_TP)], axis=1)
-    projected = jnp.dot(rows_att, wout_buf[...].reshape(1024, 1024), preferred_element_type=F32)
-    own_rows = pl.ds(pl.multiple_of(tp * 64, 64), 64)
-    own_tokens = jnp.concatenate([tok_buf[t, own_rows, :] for t in range(N_TP)], axis=1)
-    res_buf[tp] = (own_tokens.astype(F32) + projected).astype(BF16)
-
-    res = Gather(
-        lambda w: res_buf.at[tp, pl.ds(w * 32, 32)],
-        lambda s, w: res_buf.at[s, pl.ds(w * 32, 32)],
-        tp_slot, z, xh, *tp_targets, sems, 66,
-    )
-    res.start()
-    res.relay_ring(False)
-    res.relay_pair()
-    res.relay_ring(True)
-    res.finish(False)
-    res.finish(True)
+    att.relay_ring(False)
+    att.relay_pair()
+    att.relay_ring(True)
+    att.finish(False)
+    att.finish(True)
     for load in loads[3:]:
         load.wait()
 
     ffn_gain = jnp.concatenate([gain_ffn[pl.ds(t, 1), :].astype(F32) for t in range(N_TP)], axis=1)
 
-    def normalise(s, _):
-        x = res_buf[s].astype(F32)
+    def residual(j):
+        rows = pl.ds(j * 256, 256)
+        attended = jnp.concatenate([att_buf[t, rows, :] for t in range(N_TP)], axis=1)
+        projected = jnp.dot(attended, wout_buf[...].reshape(1024, 1024), preferred_element_type=F32)
+        held = jnp.concatenate([tok_buf[t, rows, :] for t in range(N_TP)], axis=1).astype(F32)
+        rounded = (held + projected).astype(BF16)
+        res_buf[rows, :] = rounded
+        x = rounded.astype(F32)
         scale = lax.rsqrt(jnp.sum(x * x, axis=1, keepdims=True) * (1.0 / 1024) + 1e-6)
-        normed_buf[pl.ds(pl.multiple_of(s * 64, 64), 64), :] = (x * scale * ffn_gain).astype(BF16)
-        return 0
-
-    lax.fori_loop(0, N_TP, normalise, 0)
+        normed_buf[rows, :] = (x * scale * ffn_gain).astype(BF16)
 
     ring_base = 80
     ring_sent = []
@@ -522,11 +500,13 @@
     def ring_last(j):
         ring_copy(j * 8 + 6, pair_rx.at[j], pair_rx.at[j], pair_at).wait_recv()
         columns = pl.ds(pl.multiple_of(tp * 128, 128), 128)
-        kept = jnp.concatenate([res_buf[4 * j + i, :, columns] for i in range(4)], axis=0).astype(F32)
+        kept = res_buf[pl.ds(j * 256, 256), columns].astype(F32)
         mixed[pl.ds(j * 256, 256), :] = (kept + own_sum(j, xh) + pair_rx[j].astype(F32)).astype(BF16)
 
+    residual(0)
     ffn(0)
     ring_first(0)
+    residual(1)
     ffn(1)
     ring_first(1)
 
@@ -536,9 +516,9 @@
     ring_third(1)
     ring_last(0)
     ring_last(1)
-    for gather in (tok, kv, wo, res):
+    for gather in (tok, kv, wo, att):
         gather.drain()
-    for copy in core_sent + swaps + ring_sent:
+    for copy in core_sent + ring_sent:
         copy.wait_send()
     for store in stores:
         store.wait()
@@ -551,7 +531,7 @@
         page = page_table[l]
         return tuple(jnp.where(page == me * PAGES_DEV + p, l, f) for p, f in enumerate(found))
 
-    found = lax.fori_loop(0, PAGES, find, (jnp.int32(-1),) * PAGES_DEV)
+    found = lax.fori_loop(0, PAGES, find, (jnp.int32(-1),) * PAGES_DEV, unroll=8)
     starts, bases = [], []
     begin, base = jnp.int32(0), jnp.int32(0)
     for r in range(REQS):
@@ -624,9 +604,8 @@
             pltpu.VMEM((2 * T, LANES), F32),
             pltpu.VMEM((2 * T, 2 * LANES), F32),
             buf(N_TP, LANES, 1024),
-            buf(N_TP, 64, LANES),
-            buf(N_TP, 64, LANES),
-            buf(N_TP, 64, 1024),
+            buf(N_TP, T, LANES),
+            buf(T, 1024),
             buf(T, 1024),
             buf(1024, T),
             buf(1024, T),

time: 98.2 us -> 91.1 us (0.928); the launches traced: 96.3 us -> 90.9 us
  Pallas kernels: 94.9 us -> 89.6 us
    pallas_call x1, Pallas kernels: 87.9 us -> 83.8 us  [per_device(): pl.pallas_call(kernel, out_shape=(jax.ShapeDtypeStruct((T, LANES), BF16),...]
    pallas_call x1, Pallas kernels: 7.03 us -> 5.8 us  [per_device(): pl.pallas_call(cache_kernel, out_shape=jax.ShapeDtypeStruct((PAGES_DEV *...]
where the time goes in v3:
time: 91.1 us; the launch traced here: 90.9 us
  Pallas kernels  89.6 us (98%)
    pallas_call x1, Pallas kernels, per_device(): pl.pallas_call(kernel, out_shape=(jax.ShapeDtypeStruct((T, LANES), BF16),...  83.8 us
    pallas_call x1, Pallas kernels, per_device(): pl.pallas_call(cache_kernel, out_shape=jax.ShapeDtypeStruct((PAGES_DEV *...  5.8 us

profile of v3, /device:TPU:48, one launch (start us, length us, event | category | flops | bytes accessed | tf_op | source)
XLA Modules:
  0.0 90.9 jit_solution(7763930036863309851)
XLA Ops:
  0.6 83.8 %layer.1 = (bf16[512,128]{1,0:T(8,128)(2,1)}, bf16[16,4,144,128]{3,2,1,0:T(8,128)(2,1)}, bf16[8192,128]{1,0:T(8,128)(2,1)}) custom-call(s32[4]{0:T(128)} %lengths.3, s32[144]{0:T(256)} %page_table.3, f32[2,2]{1,0:T(2,128)} %var_bias.1, bf16[512,128]{1,0:T(8,128)(2,1)} %tokens.1, s32[4,128]{1,0:T(4,128)} %bitcast.6, s32[4,128]{1,0:T(4,128)} %bitcast.7, ...), custom_call_target="tpu_custom_call" | custom-call | tf_op jit(solution)/shard_map/layer/pallas_call | solution.py:589
  84.4 0.0 copy-start
  84.4 5.8 %pages.1 = bf16[576,2,128]{2,1,0:T(2,128)(2,1)} custom-call(s32[4]{0:T(128)} %lengths.3, s32[144]{0:T(256)} %page_table.3, bf16[64,144,128]{2,1,0:T(8,128)(2,1)} %bitcast.5, bf16[8192,128]{1,0:T(8,128)(2,1)} %get-tuple-element.7.v_all), custom_call_target="tpu_custom_call" | custom-call | tf_op jit(solution)/shard_map/pages/pallas_call | solution.py:630
  90.2 0.0 copy-done
  90.2 0.7 copy.18
Async XLA Ops:
  84.4 5.8 %copy-start = (bf16[512,128]{1,0:T(8,128)(2,1)S(1)}, bf16[512,128]{1,0:T(8,128)(2,1)}, u32[]{:S(2)}) copy-start(bf16[512,128]{1,0:T(8,128)(2,1)} %get-tuple-element.10) | copy-start | bytes 393220
